TPU v7x, 128 devices: a whole 4x4x4 slice. The times are simulated.
128 devices in a mesh: row: 8 (over y, x_hi), col: 16 (over x_lo, z, core).
Axes of the slice: x: 4 (x_hi: 2, x_lo: 2; x = x_hi * 2 + x_lo), y: 4, z: 4, core: 2. Of those that a mesh axis runs over, the one named last changes fastest.
Arguments:
- local_ops: bfloat16 [8, 16, 2048, 2048], P('row', 'col'), may hold values from -2 to 30, as said below
- loads: float32 [8, 16, 2048, 256], P('row', 'col'), may hold values from -6 to 6
- modes: float32 [8, 16, 32, 2048], P('row', 'col'), may hold values from -1 to 1
- coarse_inverse: float32 [4096, 4096], P('row', 'col'), may hold values from -1 to 1
- face_rows: int32 [8, 16, 4, 512], P('row', 'col'), may hold values from 0 to 2047, as said below
- adjacency: int32 [8, 16, 4], P('row', 'col'), may hold values from 0 to 1, as said below
- contact: int32 [8, 16, 2048], P('row', 'col'), may hold values 0 or 1
Outputs:
- multipliers: float32 [8, 16, 2048, 256], P('row', 'col')
Inputs may be any that keep to these rules, and one draw needn't show every extreme that they name: `face_rows`: for each subdomain the 2048 entries are a permutation of 0 to 2047. `adjacency`: symmetric across each shared face (a subdomain's south flag equals the north flag of the one below it, its east flag the west flag of the one to its right); 0 on faces at the grid's edge. `local_ops`: each subdomain's local dual operator is symmetric positive definite.
All inputs are finite; a program needn't handle non-finite values. No bound on the sum of `contact` on one device may be relied on, other than what follows from the above.
Results may differ from a plain program's by a relative error of at most 0.00099.
Values sent between devices are 32-bit elements; how exact they have to be, the bound alone decides.
A program may use at most 128 MiB of HBM per device.

v0:
```python
import functools
import jax
import jax.numpy as jnp
from jax import lax
from jax.sharding import Mesh
from jax.sharding import PartitionSpec as P

ITERS = 2
ROW = ("row_0", "row_1")
COL = ("col_0", "col_1", "col_2")
ROW_COL = ("row_0", "row_1", "col_0", "col_1", "col_2")


def extended(block, sides, width):
    for axis, dim in sides:
        count = lax.axis_size(axis)
        forward = [(i, i + 1) for i in range(count - 1)]
        backward = [(target, source) for source, target in forward]
        low = lax.ppermute(
            lax.slice_in_dim(block, block.shape[dim] - width, None, axis=dim), axis, forward
        )
        high = lax.ppermute(lax.slice_in_dim(block, 0, width, axis=dim), axis, backward)
        block = jnp.concatenate([low, block, high], axis=dim)
    return block


def in_blocks(value, dim, devices):
    shape = value.shape
    blocks = value.reshape(*shape[:dim], devices, shape[dim] // devices, *shape[dim + 1 :])
    return jnp.moveaxis(blocks, dim, 0)


def summed_on_arrival(value, axis, dim):
    blocks = in_blocks(value, dim, lax.axis_size(axis))
    arrived = lax.all_to_all(blocks, axis, split_axis=0, concat_axis=0, tiled=True)
    return arrived.sum(axis=0)


def by_axis(value, axes):
    return functools.reduce(lax.psum, axes, value)


def per_device(local_ops, loads, modes, coarse_inverse, face_rows, adjacency, contact):
    local_op = local_ops[0, 0]
    load_term = loads[0, 0]
    mode_rows = modes[0, 0]
    row_index = face_rows[0, 0]
    adj_flags = adjacency[0, 0].astype(jnp.float32)
    face_size = row_index.shape[1]
    order = load_term.shape[0]
    case_count = load_term.shape[1]
    flat_rows = row_index.reshape(-1)
    free_face = jnp.repeat(1.0 - adj_flags, face_size)
    row_free = jnp.zeros((order,), jnp.float32).at[flat_rows].set(free_face)
    weight = 0.5 + 0.5 * row_free
    clamp_rows = contact[0, 0].astype(jnp.float32) * row_free > 0.5

    def assemble(field_values):
        blocks = jnp.take(field_values, row_index, axis=0)
        vertical = extended(blocks[0:2], ((ROW, 0),), 1)
        lateral = extended(blocks[2:4], ((COL, 0),), 1)
        incoming = (
            jnp.stack([vertical[0], vertical[3], lateral[0], lateral[3]]) * adj_flags[:, None, None]
        )
        return field_values.at[flat_rows].add(incoming.reshape(-1, case_count))

    multipliers = jnp.zeros((order, case_count), jnp.float32)
    for iteration in range(ITERS):
        if iteration == 0:
            local_term = -load_term
        else:
            local_term = (
                jnp.dot(
                    local_op, multipliers.astype(jnp.bfloat16), preferred_element_type=jnp.float32
                )
                - load_term
            )
        gradient = assemble(local_term)
        coarse_coef = jnp.dot(
            mode_rows, gradient, precision=lax.Precision.HIGHEST, preferred_element_type=jnp.float32
        )
        tile_cols = coarse_inverse.shape[1]
        col_index = lax.axis_index(COL)
        gathered = lax.all_gather(coarse_coef, ROW_COL, axis=0, tiled=True)
        coarse_block = lax.dynamic_slice_in_dim(gathered, col_index * tile_cols, tile_cols, 0)
        coarse_amount = summed_on_arrival(
            jnp.dot(
                coarse_inverse,
                coarse_block,
                precision=lax.Precision.HIGHEST,
                preferred_element_type=jnp.float32,
            ),
            COL,
            0,
        )
        correction = lax.dot_general(
            mode_rows,
            coarse_amount,
            (((0,), (0,)), ((), ())),
            precision=lax.Precision.HIGHEST,
            preferred_element_type=jnp.float32,
        )
        direction = gradient - assemble(correction)
        direction_half = direction.astype(jnp.bfloat16)
        operated = jnp.dot(local_op, direction_half, preferred_element_type=jnp.float32)
        totals = (
            by_axis(jnp.sum(weight[:, None] * direction * direction, axis=0), ROW_COL),
            by_axis(jnp.sum(direction * operated, axis=0), ROW_COL),
        )
        step_length = totals[0] / totals[1]
        multipliers = multipliers - step_length[None, :] * direction
        multipliers = jnp.where(clamp_rows[:, None], jnp.maximum(multipliers, 0.0), multipliers)
    return multipliers[None, None]


def solution(mesh):
    torus = Mesh(mesh.devices.reshape(4, 2, 2, 4, 2), ("row_0", "row_1", "col_0", "col_1", "col_2"))
    return jax.shard_map(
        per_device,
        mesh=torus,
        in_specs=(
            P(ROW, COL, None, None),
            P(ROW, COL, None, None),
            P(ROW, COL, None, None),
            P(ROW, COL),
            P(ROW, COL, None, None),
            P(ROW, COL, None),
            P(ROW, COL, None),
        ),
        out_specs=P(ROW, COL, None, None),
        check_vma=False,
    )
```

profile of v0, /device:TPU:1, one launch (start us, length us, event | category | flops | bytes accessed | tf_op | source)
XLA Modules:
  0.0 553.5 jit_solution(13121661826302791065)
XLA Ops:
  8.0 1.9 copy.43
  12.8 1.9 copy.45
  14.7 8.6 %gather_fusion = f32[2048,256]{1,0:T(8,128)} fusion(f32[2048,256]{1,0:T(8,128)S(1)} %copy.45, s32[2048]{0:T(1024)S(1)} %broadcast_clamp_fusion), kind=kCustom, calls=%fused_computation.clone | custom fusion | bytes 4202496 | tf_op jit(solution)/shard_map/jit(_take)/gather | solution.py:59
  23.3 1.9 broadcast_select_fusion.3
  25.4 5.5 collective-permute-start
  32.2 4.4 collective-permute-start.2
  36.6 1.9 collective-permute-start.3
  38.6 2.8 collective-permute-done
  41.4 13.2 %collective-permute-done.1 = f32[1,512,256]{2,1,0:T(8,128)S(1)} collective-permute-done((f32[1,512,256]{2,1,0:T(8,128)S(1)}, f32[1,512,256]{2,1,0:T(8,128)S(1)}, u32[]{:S(2)}, u32[]{:S(2)}) %collective-permute-start.1) | collective-permute-done | bytes 524320 | tf_op jit(solution)/shard_map/ppermute | solution.py:22
  56.5 12.7 %scatter_fusion = f32[2048,256]{1,0:T(8,128)S(1)} fusion(f32[2048,256]{1,0:T(8,128)S(1)} %copy.45, s32[2048]{0:T(1024)S(1)} %bitcast.116, f32[2048,256]{1,0:T(8,128)} %bitcast_multiply_fusion.3), kind=kCustom, calls=%fused_computation.5 | custom fusion | flops 524288 | bytes 6299648 | tf_op jit(solution)/shard_map/scatter-add | solution.py:65
  71.1 73.4 %all-gather.3.cloned.1.call-done = f32[4096,256]{1,0:T(8,128)} async-done(((f32[32,256]{1,0:T(8,128)}), f32[4096,256]{1,0:T(8,128)}) %all-gather.3.cloned.1.call-update) | async-done | bytes 4194320 | tf_op jit(solution)/shard_map/all_gather | solution.py:84
  144.5 2.0 convolution_bitcast_fusion.3
  147.5 3.6 all-to-all-start
  151.2 9.7 %all-to-all-done = f32[16,32,256]{2,1,0:T(8,128)S(1)} async-done(((f32[16,32,256]{2,1,0:T(8,128)}), f32[16,32,256]{2,1,0:T(8,128)S(1)}, u32[]{:S(2)}, u32[]{:S(2)}) %all-to-all-start) | async-done | bytes 524320 | tf_op jit(solution)/shard_map/all_to_all | solution.py:35
  161.0 3.1 convolution_bitcast_fusion.1
  164.1 2.9 copy.48
  167.0 10.1 %gather_fusion.1 = f32[2048,256]{1,0:T(8,128)} fusion(f32[2048,256]{1,0:T(8,128)} %copy.48, s32[2048]{0:T(1024)S(1)} %broadcast_clamp_fusion), kind=kCustom, calls=%fused_computation.1.clone | custom fusion | bytes 4202496 | tf_op jit(solution)/shard_map/jit(_take)/gather | solution.py:59
  177.2 1.9 broadcast_select_fusion.2
  180.3 4.5 collective-permute-start.4
  186.1 1.9 collective-permute-start.6
  188.0 3.6 collective-permute-start.7
  191.7 8.5 %scatter_custom_fusion = f32[2048]{0:T(1024)S(1)} fusion(s32[2048]{0:T(1024)S(1)} %bitcast.117, f32[2048]{0:T(1024)S(1)} %bitcast.128, f32[]{:T(128)} %constant.19.clone.1), kind=kCustom, calls=%fused_computation.70 | custom fusion | bytes 8196 | tf_op jit(solution)/shard_map/scatter | solution.py:54
  202.1 5.0 collective-permute-done.5
  211.1 12.7 %scatter_fusion.1 = f32[2048,256]{1,0:T(8,128)S(1)} fusion(f32[2048,256]{1,0:T(8,128)S(1)} %copy-done.1, s32[2048]{0:T(1024)S(1)} %bitcast.118, f32[2048,256]{1,0:T(8,128)} %bitcast_multiply_fusion.2), kind=kCustom, calls=%fused_computation.6 | custom fusion | flops 524288 | bytes 6299648 | tf_op jit(solution)/shard_map/scatter-add | solution.py:65
  223.8 1.9 copy.50
  225.7 2.6 fusion.24
  228.3 6.7 %fusion.31 = f32[256]{0:T(256)S(1)} fusion(f32[2048,256]{0,1:T(8,128)S(1)} %get-tuple-element.29, bf16[1,1,2048,2048]{3,2,1,0:T(8,128)(2,1)} %param.9), kind=kOutput, calls=%fused_computation.41 | convolution fusion | flops 2149056256 | bytes 10486784 | tf_op jit(solution)/shard_map/dot_general | solution.py:105
  235.0 7.0 %all-reduce.3 = (f32[256]{0:T(256)S(1)}, f32[256]{0:T(256)S(1)}) all-reduce(f32[256]{0:T(256)S(1)} %get-tuple-element.28, f32[256]{0:T(256)S(1)} %fusion.31), channel_id=1, replica_groups=mesh['row_0'=4,'row_1'=2,'col_0'=2,'col_1'=4,'col_2'=2] {'row_0'}, use_global_device_ids=true, to_apply=%region_5.7 | all-reduce | flops 512 | bytes 4096 | tf_op jit(solution)/shard_map/psum | solution.py:40
  242.0 5.3 all-reduce.9
  247.3 4.6 all-reduce.7
  251.9 14.5 %all-reduce.1 = (f32[256]{0:T(256)S(1)}, f32[256]{0:T(256)S(1)}) all-reduce(f32[256]{0:T(256)S(1)} %get-tuple-element.20, f32[256]{0:T(256)S(1)} %get-tuple-element.21), channel_id=1, replica_groups=mesh['row_0'=4,'row_1'=2,'col_0'=2,'col_1'=4,'col_2'=2] {'col_1'}, use_global_device_ids=true, to_apply=%region_8.10 | all-reduce | flops 512 | bytes 4096 | tf_op jit(solution)/shard_map/psum | solution.py:40
  266.4 7.1 %all-reduce.5 = (f32[256]{0:T(256)S(1)}, f32[256]{0:T(256)S(1)}) all-reduce(f32[256]{0:T(256)S(1)} %get-tuple-element.8, f32[256]{0:T(256)S(1)} %get-tuple-element.9), channel_id=1, replica_groups=mesh['row_0'=4,'row_1'=2,'col_0'=2,'col_1'=4,'col_2'=2] {'col_2'}, use_global_device_ids=true, to_apply=%region_9.11 | all-reduce | flops 512 | bytes 4096 | tf_op jit(solution)/shard_map/psum | solution.py:40
  273.5 7.7 %fusion.21 = f32[2048,256]{0,1:T(8,128)} fusion(bf16[1,1,2048,2048]{3,2,1,0:T(8,128)(2,1)} %param.9, f32[1,1,2048,256]{2,3,1,0:T(8,128)S(1)} %copy-done.4, f32[2048,256]{0,1:T(8,128)} %copy-done.5, f32[256]{0:T(256)S(1)} %div.6, pred[2048]{0:T(1024)(128)(4,1)S(1)} %multiply_compare_fusion), kind=kOutput, calls=%fused_computation.26 | convolution fusion | flops 2150629376 | bytes 14683136 | tf_op jit(solution)/shard_map/dot_general | solution.py:73
  281.2 1.9 copy.52
  283.1 8.6 %gather_fusion.2 = f32[2048,256]{1,0:T(8,128)} fusion(f32[2048,256]{1,0:T(8,128)S(1)} %copy.52, s32[2048]{0:T(1024)S(1)} %broadcast_clamp_fusion), kind=kCustom, calls=%fused_computation.2.clone | custom fusion | bytes 4202496 | tf_op jit(solution)/shard_map/jit(_take)/gather | solution.py:59
  291.8 1.9 broadcast_select_fusion.1
  293.8 3.9 collective-permute-start.10
  297.7 1.9 collective-permute-start.11
  299.6 2.6 collective-permute-start.8
  303.8 4.4 collective-permute-done.11
  308.2 4.1 collective-permute-done.8
  312.3 13.2 %collective-permute-done.9 = f32[1,512,256]{2,1,0:T(8,128)S(1)} collective-permute-done((f32[1,512,256]{2,1,0:T(8,128)S(1)}, f32[1,512,256]{2,1,0:T(8,128)S(1)}, u32[]{:S(2)}, u32[]{:S(2)}) %collective-permute-start.9) | collective-permute-done | bytes 524320 | tf_op jit(solution)/shard_map/ppermute | solution.py:22
  327.3 12.9 %scatter_fusion.2 = f32[2048,256]{1,0:T(8,128)S(1)} fusion(f32[2048,256]{1,0:T(8,128)S(1)} %copy.52, s32[2048]{0:T(1024)S(1)} %bitcast.119, f32[2048,256]{1,0:T(8,128)} %bitcast_multiply_fusion.1), kind=kCustom, calls=%fused_computation.7 | custom fusion | flops 524288 | bytes 6299648 | tf_op jit(solution)/shard_map/scatter-add | solution.py:65
  342.0 70.5 %all-gather.5.cloned.1.call-done = f32[4096,256]{1,0:T(8,128)} async-done(((f32[32,256]{1,0:T(8,128)}), f32[4096,256]{1,0:T(8,128)}) %all-gather.5.cloned.1.call-update) | async-done | bytes 4194320 | tf_op jit(solution)/shard_map/all_gather | solution.py:84
  412.5 2.0 convolution_bitcast_fusion.2
  415.5 13.4 %all_to_all.10 = f32[16,32,256]{2,1,0:T(8,128)S(1)} all-to-all(f32[16,32,256]{2,1,0:T(8,128)} %bitcast.115), channel_id=1, replica_groups=mesh['row_0'=4,'row_1'=2,'col_0'=2,'col_1'=4,'col_2'=2] {'col_0','col_1'..., dimensions={0} | all-to-all | bytes 1048576 | tf_op jit(solution)/shard_map/all_to_all | solution.py:35
  428.9 3.2 convolution_bitcast_fusion
  432.1 2.9 copy.55
  435.0 10.2 %gather_fusion.3 = f32[2048,256]{1,0:T(8,128)} fusion(f32[2048,256]{1,0:T(8,128)} %copy.55, s32[2048]{0:T(1024)S(1)} %broadcast_clamp_fusion), kind=kCustom, calls=%fused_computation.3.clone | custom fusion | bytes 4202496 | tf_op jit(solution)/shard_map/jit(_take)/gather | solution.py:59
  445.2 1.9 broadcast_select_fusion
  448.3 4.5 collective-permute-start.12
  454.1 1.9 collective-permute-start.14
  456.1 3.6 collective-permute-start.15
  462.4 12.8 %collective-permute-done.13 = f32[1,512,256]{2,1,0:T(8,128)} collective-permute-done((f32[1,512,256]{2,1,0:T(8,128)}, f32[1,512,256]{2,1,0:T(8,128)}, u32[]{:S(2)}, u32[]{:S(2)}) %collective-permute-start.13) | collective-permute-done | bytes 524320 | tf_op jit(solution)/shard_map/ppermute | solution.py:22
  479.1 12.9 %scatter_fusion.3 = f32[2048,256]{1,0:T(8,128)S(1)} fusion(f32[2048,256]{1,0:T(8,128)S(1)} %copy-done.2, s32[2048]{0:T(1024)S(1)} %bitcast.120, f32[2048,256]{1,0:T(8,128)} %bitcast_multiply_fusion), kind=kCustom, calls=%fused_computation.8 | custom fusion | flops 524288 | bytes 6299648 | tf_op jit(solution)/shard_map/scatter-add | solution.py:65
  492.0 1.9 copy.57
  493.9 2.6 fusion.25
  496.5 6.7 %fusion.28 = f32[256]{0:T(256)S(1)} fusion(f32[2048,256]{0,1:T(8,128)S(1)} %get-tuple-element.27, bf16[1,1,2048,2048]{3,2,1,0:T(8,128)(2,1)} %param.9), kind=kOutput, calls=%fused_computation.40 | convolution fusion | flops 2149056256 | bytes 10486784 | tf_op jit(solution)/shard_map/dot_general | solution.py:105
  503.2 7.0 %all-reduce.2 = (f32[256]{0:T(256)S(1)}, f32[256]{0:T(256)S(1)}) all-reduce(f32[256]{0:T(256)S(1)} %get-tuple-element.26, f32[256]{0:T(256)S(1)} %fusion.28), channel_id=1, replica_groups=mesh['row_0'=4,'row_1'=2,'col_0'=2,'col_1'=4,'col_2'=2] {'row_0'}, use_global_device_ids=true, to_apply=%region_20.22 | all-reduce | flops 512 | bytes 4096 | tf_op jit(solution)/shard_map/psum | solution.py:40
  510.2 5.3 all-reduce.8
  515.5 4.6 all-reduce.6
  520.1 14.5 %all-reduce = (f32[256]{0:T(256)S(1)}, f32[256]{0:T(256)S(1)}) all-reduce(f32[256]{0:T(256)S(1)} %get-tuple-element.18, f32[256]{0:T(256)S(1)} %get-tuple-element.19), channel_id=1, replica_groups=mesh['row_0'=4,'row_1'=2,'col_0'=2,'col_1'=4,'col_2'=2] {'col_1'}, use_global_device_ids=true, to_apply=%region_23.25 | all-reduce | flops 512 | bytes 4096 | tf_op jit(solution)/shard_map/psum | solution.py:40
  534.5 7.1 %all-reduce.4 = (f32[256]{0:T(256)S(1)}, f32[256]{0:T(256)S(1)}) all-reduce(f32[256]{0:T(256)S(1)} %get-tuple-element.6, f32[256]{0:T(256)S(1)} %get-tuple-element.7), channel_id=1, replica_groups=mesh['row_0'=4,'row_1'=2,'col_0'=2,'col_1'=4,'col_2'=2] {'col_2'}, use_global_device_ids=true, to_apply=%region_24.26 | all-reduce | flops 512 | bytes 4096 | tf_op jit(solution)/shard_map/psum | solution.py:40
  541.7 3.0 fusion.26
  (78 shorter events, 36.1 us)
Async XLA Ops:
  6.5 138.0 %copy-start = (f32[512,256]{1,0:T(8,128)S(1)}, f32[512,256]{1,0:T(8,128)}, u32[]{:S(2)}) copy-start(f32[512,256]{1,0:T(8,128)} %param.12) | copy-start | bytes 1572868
  6.5 138.0 %all-gather.3.cloned.1.call-start = ((), (), s32[]{:S(2)}) async-start(), calls=%async_computation.2 | async-start | bytes 4227072 | tf_op jit(solution)/shard_map/all_gather | solution.py:84
  10.0 1.3 copy-start.3
  25.2 13.3 %copy-start.10 = (s32[1,1,4]{2,1,0:T(1,128)S(1)}, s32[1,1,4]{2,1,0:T(1,128)}, u32[]{:S(2)}) copy-start(s32[1,1,4]{2,1,0:T(1,128)} %param.14) | copy-start | bytes 52
  25.2 13.4 %copy-start.8 = (s32[1,1,4,512]{3,2,1,0:T(4,128)S(1)}, s32[1,1,4,512]{3,2,1,0:T(4,128)}, u32[]{:S(2)}) copy-start(s32[1,1,4,512]{3,2,1,0:T(4,128)} %param.13) | copy-start | bytes 24580
  25.4 16.1 %collective-permute-start = (f32[1,512,256]{2,1,0:T(8,128)S(1)}, f32[1,512,256]{2,1,0:T(8,128)S(1)}, u32[]{:S(2)}, u32[]{:S(2)}) collective-permute-start(f32[1,512,256]{2,1,0:T(8,128)S(1)} %get-tuple-element.42), channel_id=1, source_target_pairs={{0,16},{16,32},{32,48},{48,64},{64,80},{80,96},{96,112},{1,17},{17... | collective-permute-start | bytes 1572872 | tf_op jit(solution)/shard_map/ppermute | solution.py:19
  30.9 23.8 %collective-permute-start.1 = (f32[1,512,256]{2,1,0:T(8,128)S(1)}, f32[1,512,256]{2,1,0:T(8,128)S(1)}, u32[]{:S(2)}, u32[]{:S(2)}) collective-permute-start(f32[1,512,256]{2,1,0:T(8,128)S(1)} %get-tuple-element.45), channel_id=1, source_target_pairs={{16,0},{32,16},{48,32},{64,48},{80,64},{96,80},{112,96},{17,1},{33... | collective-permute-start | bytes 1572872 | tf_op jit(solution)/shard_map/ppermute | solution.py:22
  32.2 22.5 %collective-permute-start.2 = (f32[1,512,256]{2,1,0:T(8,128)S(1)}, f32[1,512,256]{2,1,0:T(8,128)S(1)}, u32[]{:S(2)}, u32[]{:S(2)}) collective-permute-start(f32[1,512,256]{2,1,0:T(8,128)S(1)} %get-tuple-element.44), channel_id=1, source_target_pairs={{0,1},{1,2},{2,3},{3,4},{4,5},{5,6},{6,7},{7,8},{8,9},{9,10},{10,1... | collective-permute-start | bytes 1572872 | tf_op jit(solution)/shard_map/ppermute | solution.py:19
  36.6 18.1 %collective-permute-start.3 = (f32[1,512,256]{2,1,0:T(8,128)S(1)}, f32[1,512,256]{2,1,0:T(8,128)S(1)}, u32[]{:S(2)}, u32[]{:S(2)}) collective-permute-start(f32[1,512,256]{2,1,0:T(8,128)S(1)} %get-tuple-element.43), channel_id=1, source_target_pairs={{1,0},{2,1},{3,2},{4,3},{5,4},{6,5},{7,6},{8,7},{9,8},{10,9},{11,1... | collective-permute-start | bytes 1572872 | tf_op jit(solution)/shard_map/ppermute | solution.py:22
  56.5 12.8 %copy-start.7 = (f32[1,1,32,2048]{3,2,1,0:T(8,128)S(1)}, f32[1,1,32,2048]{3,2,1,0:T(8,128)}, u32[]{:S(2)}) copy-start(f32[1,1,32,2048]{3,2,1,0:T(8,128)} %param.11) | copy-start | bytes 786436
  147.5 13.4 %all-to-all-start = ((f32[16,32,256]{2,1,0:T(8,128)}), f32[16,32,256]{2,1,0:T(8,128)S(1)}, u32[]{:S(2)}, u32[]{:S(2)}) async-start(f32[16,32,256]{2,1,0:T(8,128)} %bitcast.114), calls=%async_computation | async-start | bytes 1048576 | tf_op jit(solution)/shard_map/all_to_all | solution.py:35
  151.2 261.3 %all-gather.5.cloned.1.call-start = ((), (), s32[]{:S(2)}) async-start(), calls=%async_computation.3 | async-start | bytes 4227072 | tf_op jit(solution)/shard_map/all_gather | solution.py:84
  179.1 21.2 %copy-start.9 = (s32[1,1,2048]{2,1,0:T(1,128)S(1)}, s32[1,1,2048]{2,1,0:T(1,128)}, u32[]{:S(2)}) copy-start(s32[1,1,2048]{2,1,0:T(1,128)} %param.15) | copy-start | bytes 24580
  180.3 21.8 %collective-permute-start.4 = (f32[1,512,256]{2,1,0:T(8,128)}, f32[1,512,256]{2,1,0:T(8,128)}, u32[]{:S(2)}, u32[]{:S(2)}) collective-permute-start(f32[1,512,256]{2,1,0:T(8,128)} %get-tuple-element.38), channel_id=1, source_target_pairs={{0,16},{16,32},{32,48},{48,64},{64,80},{80,96},{96,112},{1,17},{17... | collective-permute-start | bytes 1572872 | tf_op jit(solution)/shard_map/ppermute | solution.py:19
  184.8 22.3 %collective-permute-start.5 = (f32[1,512,256]{2,1,0:T(8,128)}, f32[1,512,256]{2,1,0:T(8,128)}, u32[]{:S(2)}, u32[]{:S(2)}) collective-permute-start(f32[1,512,256]{2,1,0:T(8,128)} %get-tuple-element.41), channel_id=1, source_target_pairs={{16,0},{32,16},{48,32},{64,48},{80,64},{96,80},{112,96},{17,1},{33... | collective-permute-start | bytes 1572872 | tf_op jit(solution)/shard_map/ppermute | solution.py:22
  186.1 21.0 %collective-permute-start.6 = (f32[1,512,256]{2,1,0:T(8,128)}, f32[1,512,256]{2,1,0:T(8,128)}, u32[]{:S(2)}, u32[]{:S(2)}) collective-permute-start(f32[1,512,256]{2,1,0:T(8,128)} %get-tuple-element.40), channel_id=1, source_target_pairs={{0,1},{1,2},{2,3},{3,4},{4,5},{5,6},{6,7},{7,8},{8,9},{9,10},{10,1... | collective-permute-start | bytes 1572872 | tf_op jit(solution)/shard_map/ppermute | solution.py:19
  188.0 19.1 %collective-permute-start.7 = (f32[1,512,256]{2,1,0:T(8,128)S(1)}, f32[1,512,256]{2,1,0:T(8,128)}, u32[]{:S(2)}, u32[]{:S(2)}) collective-permute-start(f32[1,512,256]{2,1,0:T(8,128)S(1)} %get-tuple-element.39), channel_id=1, source_target_pairs={{1,0},{2,1},{3,2},{4,3},{5,4},{6,5},{7,6},{8,7},{9,8},{10,9},{11,1... | collective-permute-start | bytes 1572872 | tf_op jit(solution)/shard_map/ppermute | solution.py:22
  208.8 2.3 copy-start.1
  228.3 6.7 %copy-start.5 = (f32[2048,256]{0,1:T(8,128)}, f32[2048,256]{0,1:T(8,128)S(1)}, u32[]{:S(2)}) copy-start(f32[2048,256]{0,1:T(8,128)S(1)} %get-tuple-element.29) | copy-start | bytes 6291460
  228.3 45.2 %copy-start.4 = (f32[1,1,2048,256]{2,3,1,0:T(8,128)S(1)}, f32[1,1,2048,256]{2,3,1,0:T(8,128)}, u32[]{:S(2)}) copy-start(f32[1,1,2048,256]{2,3,1,0:T(8,128)} %copy-done.3) | copy-start | bytes 6291460
  293.8 10.0 %collective-permute-start.10 = (f32[1,512,256]{2,1,0:T(8,128)S(1)}, f32[1,512,256]{2,1,0:T(8,128)S(1)}, u32[]{:S(2)}, u32[]{:S(2)}) collective-permute-start(f32[1,512,256]{2,1,0:T(8,128)S(1)} %get-tuple-element.36), channel_id=1, source_target_pairs={{0,1},{1,2},{2,3},{3,4},{4,5},{5,6},{6,7},{7,8},{8,9},{9,10},{10,1... | collective-permute-start | bytes 1572872 | tf_op jit(solution)/shard_map/ppermute | solution.py:19
  297.7 10.5 %collective-permute-start.11 = (f32[1,512,256]{2,1,0:T(8,128)S(1)}, f32[1,512,256]{2,1,0:T(8,128)S(1)}, u32[]{:S(2)}, u32[]{:S(2)}) collective-permute-start(f32[1,512,256]{2,1,0:T(8,128)S(1)} %get-tuple-element.35), channel_id=1, source_target_pairs={{1,0},{2,1},{3,2},{4,3},{5,4},{6,5},{7,6},{8,7},{9,8},{10,9},{11,1... | collective-permute-start | bytes 1572872 | tf_op jit(solution)/shard_map/ppermute | solution.py:22
  299.6 12.7 %collective-permute-start.8 = (f32[1,512,256]{2,1,0:T(8,128)S(1)}, f32[1,512,256]{2,1,0:T(8,128)S(1)}, u32[]{:S(2)}, u32[]{:S(2)}) collective-permute-start(f32[1,512,256]{2,1,0:T(8,128)S(1)} %get-tuple-element.34), channel_id=1, source_target_pairs={{0,16},{16,32},{32,48},{48,64},{64,80},{80,96},{96,112},{1,17},{17... | collective-permute-start | bytes 1572872 | tf_op jit(solution)/shard_map/ppermute | solution.py:19
  302.2 23.3 %collective-permute-start.9 = (f32[1,512,256]{2,1,0:T(8,128)S(1)}, f32[1,512,256]{2,1,0:T(8,128)S(1)}, u32[]{:S(2)}, u32[]{:S(2)}) collective-permute-start(f32[1,512,256]{2,1,0:T(8,128)S(1)} %get-tuple-element.37), channel_id=1, source_target_pairs={{16,0},{32,16},{48,32},{64,48},{80,64},{96,80},{112,96},{17,1},{33... | collective-permute-start | bytes 1572872 | tf_op jit(solution)/shard_map/ppermute | solution.py:22
  448.3 14.1 %collective-permute-start.12 = (f32[1,512,256]{2,1,0:T(8,128)}, f32[1,512,256]{2,1,0:T(8,128)}, u32[]{:S(2)}, u32[]{:S(2)}) collective-permute-start(f32[1,512,256]{2,1,0:T(8,128)} %get-tuple-element.30), channel_id=1, source_target_pairs={{0,16},{16,32},{32,48},{48,64},{64,80},{80,96},{96,112},{1,17},{17... | collective-permute-start | bytes 1572872 | tf_op jit(solution)/shard_map/ppermute | solution.py:19
  452.8 22.3 %collective-permute-start.13 = (f32[1,512,256]{2,1,0:T(8,128)}, f32[1,512,256]{2,1,0:T(8,128)}, u32[]{:S(2)}, u32[]{:S(2)}) collective-permute-start(f32[1,512,256]{2,1,0:T(8,128)} %get-tuple-element.33), channel_id=1, source_target_pairs={{16,0},{32,16},{48,32},{64,48},{80,64},{96,80},{112,96},{17,1},{33... | collective-permute-start | bytes 1572872 | tf_op jit(solution)/shard_map/ppermute | solution.py:22
  454.1 21.0 %collective-permute-start.14 = (f32[1,512,256]{2,1,0:T(8,128)}, f32[1,512,256]{2,1,0:T(8,128)}, u32[]{:S(2)}, u32[]{:S(2)}) collective-permute-start(f32[1,512,256]{2,1,0:T(8,128)} %get-tuple-element.32), channel_id=1, source_target_pairs={{0,1},{1,2},{2,3},{3,4},{4,5},{5,6},{6,7},{7,8},{8,9},{9,10},{10,1... | collective-permute-start | bytes 1572872 | tf_op jit(solution)/shard_map/ppermute | solution.py:19
  456.1 19.1 %collective-permute-start.15 = (f32[1,512,256]{2,1,0:T(8,128)S(1)}, f32[1,512,256]{2,1,0:T(8,128)}, u32[]{:S(2)}, u32[]{:S(2)}) collective-permute-start(f32[1,512,256]{2,1,0:T(8,128)S(1)} %get-tuple-element.31), channel_id=1, source_target_pairs={{1,0},{2,1},{3,2},{4,3},{5,4},{6,5},{7,6},{8,7},{9,8},{10,9},{11,1... | collective-permute-start | bytes 1572872 | tf_op jit(solution)/shard_map/ppermute | solution.py:22
  476.8 2.3 copy-start.2
  496.5 6.7 %copy-start.6 = (f32[2048,256]{0,1:T(8,128)}, f32[2048,256]{0,1:T(8,128)S(1)}, u32[]{:S(2)}) copy-start(f32[2048,256]{0,1:T(8,128)S(1)} %get-tuple-element.27) | copy-start | bytes 6291460
Sparse Core Ops, SparseCore 0:
  71.2 73.2 all-gather.2
  342.1 70.3 all-gather.4
where the time goes:
time: 563 us; the launch traced here: 554 us
  waiting for transfers between devices  210 us (37%)
  blocking collectives  90.3 us (16%)
  other arithmetic  80.6 us (14%)
  local copies, waits for them, and re-layouts  74.2 us (13%)
  starting transfers between devices  49.1 us (9%)
  matrix products  35 us (6%)
  between operations  14.1 us (3%)
    all_gather x2, waiting for transfers between devices, per_device(): gathered = lax.all_gather(coarse_coef, ROW_COL, axis=0, tiled=True)  144 us
    psum x10, blocking collectives, by_axis(): return functools.reduce(lax.psum, axes, value)  76.9 us
    scatter-add x4, other arithmetic, assemble(): return field_values.at[flat_rows].add(incoming.reshape(-1, case_count))  51.3 us
    ppermute x8, waiting for transfers between devices, extended(): lax.ppermute(lax.slice_in_dim(block, 0, width, axis=dim), axis, backward)  48.5 us
    gather x4, local copies, waits for them, and re-layouts, assemble(): blocks = jnp.take(field_values, row_index, axis=0)  37.5 us
    ppermute x8, starting transfers between devices, extended(): lax.ppermute(lax.slice_in_dim(block, block.shape[dim] - width, None, axis...  29.2 us
    ppermute x8, starting transfers between devices, extended(): lax.ppermute(lax.slice_in_dim(block, 0, width, axis=dim), axis, backward)  16.2 us
    all_to_all x1, blocking collectives, summed_on_arrival(): lax.all_to_all(blocks, axis, split_axis=0, concat_axis=0, tiled=True)  13.4 us
  transfers between devices with their start and end apart: 19, of which 12 were waited for; matrix products, arithmetic and copies ran while one was open for 2% of the time, Pallas kernels for 0%

commit v1 on v0

--- a/solution.py
+++ b/solution.py
@@ -81,7 +81,13 @@
         )
         tile_cols = coarse_inverse.shape[1]
         col_index = lax.axis_index(COL)
-        gathered = lax.all_gather(coarse_coef, ROW_COL, axis=0, tiled=True)
+        _store_shapes = lambda point: jnp.concatenate(
+            lax.all_to_all(
+                jnp.stack([point for _ in range(lax.axis_size(ROW_COL))], 0), ROW_COL, 0, 0
+            ),
+            0,
+        )
+        gathered = _store_shapes(coarse_coef)
         coarse_block = lax.dynamic_slice_in_dim(gathered, col_index * tile_cols, tile_cols, 0)
         coarse_amount = summed_on_arrival(
             jnp.dot(

time: 563 us -> 534 us (0.948)
  waiting for transfers between devices: 210 us -> 117 us
  blocking collectives: 90.3 us -> 150 us
  starting transfers between devices: 49.1 us -> 67.2 us
  between operations: 14.1 us -> 0.71 us
    all_gather x2 -> x0, waiting for transfers between devices: 144 us -> none  [per_device(): gathered = lax.all_gather(coarse_coef, ROW_COL, axis=0, tiled=True)]
    all_to_all x0 -> x1, blocking collectives: none -> 63 us  [per_device(): lax.all_to_all(jnp.stack([point for _ in range(lax.axis_size(ROW_COL))],...]
    all_to_all x0 -> x1, waiting for transfers between devices: none -> 52.2 us  [per_device(): lax.all_to_all(jnp.stack([point for _ in range(lax.axis_size(ROW_COL))],...]
    all_to_all x0 -> x1, starting transfers between devices: none -> 16.7 us  [per_device(): lax.all_to_all(jnp.stack([point for _ in range(lax.axis_size(ROW_COL))],...]
  transfers between devices with their start and end apart: 19 -> 18, of which waited for: 12 -> 15; matrix products, arithmetic and copies ran while one was open for 2% -> 2% of each run, Pallas kernels for 0% -> 0%
where the time goes in v1:
time: 534 us; the launch traced here: 524 us
  blocking collectives  150 us (28%)
  waiting for transfers between devices  117 us (22%)
  other arithmetic  80.6 us (15%)
  local copies, waits for them, and re-layouts  76.6 us (14%)
  starting transfers between devices  67.2 us (13%)
  matrix products  32.8 us (6%)
    psum x10, blocking collectives, by_axis(): return functools.reduce(lax.psum, axes, value)  72.3 us
    all_to_all x1, blocking collectives, per_device(): lax.all_to_all(jnp.stack([point for _ in range(lax.axis_size(ROW_COL))],...  63 us
    all_to_all x1, waiting for transfers between devices, per_device(): lax.all_to_all(jnp.stack([point for _ in range(lax.axis_size(ROW_COL))],...  52.2 us
    scatter-add x4, other arithmetic, assemble(): return field_values.at[flat_rows].add(incoming.reshape(-1, case_count))  51.3 us
    ppermute x8, waiting for transfers between devices, extended(): lax.ppermute(lax.slice_in_dim(block, 0, width, axis=dim), axis, backward)  43.9 us
    gather x4, local copies, waits for them, and re-layouts, assemble(): blocks = jnp.take(field_values, row_index, axis=0)  37.5 us
    ppermute x8, starting transfers between devices, extended(): lax.ppermute(lax.slice_in_dim(block, block.shape[dim] - width, None, axis...  27.7 us
    ppermute x8, starting transfers between devices, extended(): lax.ppermute(lax.slice_in_dim(block, 0, width, axis=dim), axis, backward)  17.9 us
  transfers between devices with their start and end apart: 18, of which 15 were waited for; matrix products, arithmetic and copies ran while one was open for 2% of the time, Pallas kernels for 0%

profile of v1, /device:TPU:1, one launch (start us, length us, event | category | flops | bytes accessed | tf_op | source)
XLA Modules:
  0.0 524.3 jit_solution(2476453764260091207)
XLA Ops:
  1.5 1.9 copy.27
  6.2 1.9 copy.29
  8.2 8.6 %gather_fusion = f32[2048,256]{1,0:T(8,128)} fusion(f32[2048,256]{1,0:T(8,128)S(1)} %copy.29, s32[2048]{0:T(1024)S(1)} %broadcast_clamp_fusion), kind=kCustom, calls=%fused_computation.clone | custom fusion | bytes 4202496 | tf_op jit(solution)/shard_map/jit(_take)/gather | solution.py:59
  16.7 1.9 broadcast_select_fusion.3
  18.8 5.5 %collective-permute-start = (f32[1,512,256]{2,1,0:T(8,128)S(1)}, f32[1,512,256]{2,1,0:T(8,128)S(1)}, u32[]{:S(2)}, u32[]{:S(2)}) collective-permute-start(f32[1,512,256]{2,1,0:T(8,128)S(1)} %get-tuple-element.42), channel_id=1, source_target_pairs={{0,16},{16,32},{32,48},{48,64},{64,80},{80,96},{96,112},{1,17},{17... | collective-permute-start | bytes 1572872 | tf_op jit(solution)/shard_map/ppermute | solution.py:19
  24.3 2.9 collective-permute-start.3
  27.2 3.4 collective-permute-start.2
  32.1 2.8 collective-permute-done
  36.8 11.3 %collective-permute-done.1 = f32[1,512,256]{2,1,0:T(8,128)S(1)} collective-permute-done((f32[1,512,256]{2,1,0:T(8,128)S(1)}, f32[1,512,256]{2,1,0:T(8,128)S(1)}, u32[]{:S(2)}, u32[]{:S(2)}) %collective-permute-start.1) | collective-permute-done | bytes 524320 | tf_op jit(solution)/shard_map/ppermute | solution.py:22
  49.9 12.7 %scatter_fusion = f32[2048,256]{1,0:T(8,128)S(1)} fusion(f32[2048,256]{1,0:T(8,128)S(1)} %copy.29, s32[2048]{0:T(1024)S(1)} %bitcast.120, f32[2048,256]{1,0:T(8,128)} %bitcast_multiply_fusion.3), kind=kCustom, calls=%fused_computation.5 | custom fusion | flops 524288 | bytes 6299648 | tf_op jit(solution)/shard_map/scatter-add | solution.py:65
  63.9 2.5 stack.22
  66.4 16.7 %all-to-all-start = ((f32[128,32,256]{2,1,0:T(8,128)}), f32[128,32,256]{2,1,0:T(8,128)}, u32[]{:S(2)}, u32[]{:S(2)}) async-start(f32[128,32,256]{2,1,0:T(8,128)} %stack.22), calls=%async_computation | async-start | bytes 8388608 | tf_op jit(solution)/shard_map/all_to_all | solution.py:85
  83.1 52.2 %all-to-all-done = f32[128,32,256]{2,1,0:T(8,128)} async-done(((f32[128,32,256]{2,1,0:T(8,128)}), f32[128,32,256]{2,1,0:T(8,128)}, u32[]{:S(2)}, u32[]{:S(2)}) %all-to-all-start) | async-done | bytes 4194336 | tf_op jit(solution)/shard_map/all_to_all | solution.py:85
  135.4 2.0 convolution_bitcast_fusion.3
  138.4 4.8 all-to-all-start.1
  143.1 9.7 %all-to-all-done.1 = f32[16,32,256]{2,1,0:T(8,128)S(1)} async-done(((f32[16,32,256]{2,1,0:T(8,128)}), f32[16,32,256]{2,1,0:T(8,128)S(1)}, u32[]{:S(2)}, u32[]{:S(2)}) %all-to-all-start.1) | async-done | bytes 524320 | tf_op jit(solution)/shard_map/all_to_all | solution.py:35
  152.9 3.1 convolution_bitcast_fusion.1
  156.1 2.9 copy.32
  159.0 10.1 %gather_fusion.1 = f32[2048,256]{1,0:T(8,128)} fusion(f32[2048,256]{1,0:T(8,128)} %copy.32, s32[2048]{0:T(1024)S(1)} %broadcast_clamp_fusion), kind=kCustom, calls=%fused_computation.1.clone | custom fusion | bytes 4202496 | tf_op jit(solution)/shard_map/jit(_take)/gather | solution.py:59
  169.1 1.9 broadcast_select_fusion.2
  172.3 3.4 collective-permute-start.4
  175.7 3.4 collective-permute-start.7
  179.1 2.1 collective-permute-start.6
  183.1 8.0 %scatter_custom_fusion = f32[2048]{0:T(1024)S(1)} fusion(s32[2048]{0:T(1024)S(1)} %bitcast.121, f32[2048]{0:T(1024)S(1)} %bitcast.132, f32[]{:T(128)} %constant.19.clone.1), kind=kCustom, calls=%fused_computation.70 | custom fusion | bytes 8196 | tf_op jit(solution)/shard_map/scatter | solution.py:54
  191.2 1.8 copy.33
  193.0 6.2 %collective-permute-done.5 = f32[1,512,256]{2,1,0:T(8,128)} collective-permute-done((f32[1,512,256]{2,1,0:T(8,128)S(1)}, f32[1,512,256]{2,1,0:T(8,128)}, u32[]{:S(2)}, u32[]{:S(2)}) %collective-permute-start.5) | collective-permute-done | bytes 524320 | tf_op jit(solution)/shard_map/ppermute | solution.py:22
  203.2 12.7 %scatter_fusion.1 = f32[2048,256]{1,0:T(8,128)S(1)} fusion(f32[2048,256]{1,0:T(8,128)S(1)} %copy-done.1, s32[2048]{0:T(1024)S(1)} %bitcast.122, f32[2048,256]{1,0:T(8,128)} %bitcast_multiply_fusion.2), kind=kCustom, calls=%fused_computation.6 | custom fusion | flops 524288 | bytes 6299648 | tf_op jit(solution)/shard_map/scatter-add | solution.py:65
  215.9 1.9 copy.34
  217.8 2.6 fusion.24
  220.4 6.7 %fusion.31 = f32[256]{0:T(256)S(1)} fusion(f32[2048,256]{0,1:T(8,128)S(1)} %get-tuple-element.29, bf16[1,1,2048,2048]{3,2,1,0:T(8,128)(2,1)} %param.9), kind=kOutput, calls=%fused_computation.41 | convolution fusion | flops 2149056256 | bytes 10486784 | tf_op jit(solution)/shard_map/dot_general | solution.py:111
  227.1 6.0 %all-reduce.3 = (f32[256]{0:T(256)S(1)}, f32[256]{0:T(256)S(1)}) all-reduce(f32[256]{0:T(256)S(1)} %get-tuple-element.28, f32[256]{0:T(256)S(1)} %fusion.31), channel_id=1, replica_groups=mesh['row_0'=4,'row_1'=2,'col_0'=2,'col_1'=4,'col_2'=2] {'row_0'}, use_global_device_ids=true, to_apply=%region_5.7 | all-reduce | flops 512 | bytes 4096 | tf_op jit(solution)/shard_map/psum | solution.py:40
  233.1 5.3 %all-reduce.9 = (f32[256]{0:T(256)S(1)}, f32[256]{0:T(256)S(1)}) all-reduce(f32[256]{0:T(256)S(1)} %get-tuple-element.12, f32[256]{0:T(256)S(1)} %get-tuple-element.13), channel_id=1, replica_groups=mesh['row_0'=4,'row_1'=2,'col_0'=2,'col_1'=4,'col_2'=2] {'row_1'}, use_global_device_ids=true, to_apply=%region_6.8 | all-reduce | flops 512 | bytes 4096 | tf_op jit(solution)/shard_map/psum | solution.py:40
  238.4 4.4 all-reduce.7
  242.8 14.1 %all-reduce.1 = (f32[256]{0:T(256)S(1)}, f32[256]{0:T(256)S(1)}) all-reduce(f32[256]{0:T(256)S(1)} %get-tuple-element.20, f32[256]{0:T(256)S(1)} %get-tuple-element.21), channel_id=1, replica_groups=mesh['row_0'=4,'row_1'=2,'col_0'=2,'col_1'=4,'col_2'=2] {'col_1'}, use_global_device_ids=true, to_apply=%region_8.10 | all-reduce | flops 512 | bytes 4096 | tf_op jit(solution)/shard_map/psum | solution.py:40
  256.9 6.4 %all-reduce.5 = (f32[256]{0:T(256)S(1)}, f32[256]{0:T(256)S(1)}) all-reduce(f32[256]{0:T(256)S(1)} %get-tuple-element.8, f32[256]{0:T(256)S(1)} %get-tuple-element.9), channel_id=1, replica_groups=mesh['row_0'=4,'row_1'=2,'col_0'=2,'col_1'=4,'col_2'=2] {'col_2'}, use_global_device_ids=true, to_apply=%region_9.11 | all-reduce | flops 512 | bytes 4096 | tf_op jit(solution)/shard_map/psum | solution.py:40
  263.3 7.7 %fusion.21 = f32[2048,256]{0,1:T(8,128)} fusion(bf16[1,1,2048,2048]{3,2,1,0:T(8,128)(2,1)} %param.9, f32[1,1,2048,256]{2,3,1,0:T(8,128)S(1)} %copy-done.4, f32[2048,256]{0,1:T(8,128)} %copy-done.5, f32[256]{0:T(256)S(1)} %div.6, pred[2048]{0:T(1024)(128)(4,1)S(1)} %multiply_compare_fusion), kind=kOutput, calls=%fused_computation.26 | convolution fusion | flops 2150629376 | bytes 14683136 | tf_op jit(solution)/shard_map/dot_general | solution.py:73
  271.0 1.9 copy.36
  272.9 8.6 %gather_fusion.2 = f32[2048,256]{1,0:T(8,128)} fusion(f32[2048,256]{1,0:T(8,128)S(1)} %copy.36, s32[2048]{0:T(1024)S(1)} %broadcast_clamp_fusion), kind=kCustom, calls=%fused_computation.2.clone | custom fusion | bytes 4202496 | tf_op jit(solution)/shard_map/jit(_take)/gather | solution.py:59
  281.6 1.9 broadcast_select_fusion.1
  283.6 4.2 collective-permute-start.8
  287.9 2.5 collective-permute-start.11
  290.4 3.5 collective-permute-start.10
  295.2 3.5 collective-permute-done.8
  300.1 12.6 %collective-permute-done.9 = f32[1,512,256]{2,1,0:T(8,128)S(1)} collective-permute-done((f32[1,512,256]{2,1,0:T(8,128)S(1)}, f32[1,512,256]{2,1,0:T(8,128)S(1)}, u32[]{:S(2)}, u32[]{:S(2)}) %collective-permute-start.9) | collective-permute-done | bytes 524320 | tf_op jit(solution)/shard_map/ppermute | solution.py:22
  314.5 12.9 %scatter_fusion.2 = f32[2048,256]{1,0:T(8,128)S(1)} fusion(f32[2048,256]{1,0:T(8,128)S(1)} %copy.36, s32[2048]{0:T(1024)S(1)} %bitcast.123, f32[2048,256]{1,0:T(8,128)} %bitcast_multiply_fusion.1), kind=kCustom, calls=%fused_computation.7 | custom fusion | flops 524288 | bytes 6299648 | tf_op jit(solution)/shard_map/scatter-add | solution.py:65
  329.1 63.0 %all_to_all.20 = f32[128,32,256]{2,1,0:T(8,128)S(1)} all-to-all(f32[128,32,256]{2,1,0:T(8,128)S(1)} %stack.27), channel_id=1, replica_groups=mesh['row_0'=4,'row_1'=2,'col_0'=2,'col_1'=4,'col_2'=2] {'row_0','row_1'..., dimensions={0} | all-to-all | bytes 8388608 | tf_op jit(solution)/shard_map/all_to_all | solution.py:85
  394.2 14.5 %all_to_all.21 = f32[16,32,256]{2,1,0:T(8,128)S(1)} all-to-all(f32[16,32,256]{2,1,0:T(8,128)} %bitcast.119), channel_id=1, replica_groups=mesh['row_0'=4,'row_1'=2,'col_0'=2,'col_1'=4,'col_2'=2] {'col_0','col_1'..., dimensions={0} | all-to-all | bytes 1048576 | tf_op jit(solution)/shard_map/all_to_all | solution.py:35
  408.8 3.2 convolution_bitcast_fusion
  411.9 2.9 copy.39
  414.8 10.2 %gather_fusion.3 = f32[2048,256]{1,0:T(8,128)} fusion(f32[2048,256]{1,0:T(8,128)} %copy.39, s32[2048]{0:T(1024)S(1)} %broadcast_clamp_fusion), kind=kCustom, calls=%fused_computation.3.clone | custom fusion | bytes 4202496 | tf_op jit(solution)/shard_map/jit(_take)/gather | solution.py:59
  425.0 1.9 broadcast_select_fusion
  428.1 3.4 collective-permute-start.12
  431.5 3.4 collective-permute-start.15
  435.0 2.1 collective-permute-start.14
  443.5 11.6 %collective-permute-done.13 = f32[1,512,256]{2,1,0:T(8,128)} collective-permute-done((f32[1,512,256]{2,1,0:T(8,128)S(1)}, f32[1,512,256]{2,1,0:T(8,128)}, u32[]{:S(2)}, u32[]{:S(2)}) %collective-permute-start.13) | collective-permute-done | bytes 524320 | tf_op jit(solution)/shard_map/ppermute | solution.py:22
  459.0 12.9 %scatter_fusion.3 = f32[2048,256]{1,0:T(8,128)S(1)} fusion(f32[2048,256]{1,0:T(8,128)S(1)} %copy-done.2, s32[2048]{0:T(1024)S(1)} %bitcast.124, f32[2048,256]{1,0:T(8,128)} %bitcast_multiply_fusion), kind=kCustom, calls=%fused_computation.8 | custom fusion | flops 524288 | bytes 6299648 | tf_op jit(solution)/shard_map/scatter-add | solution.py:65
  473.8 2.6 fusion.25
  476.4 6.7 %fusion.28 = f32[256]{0:T(256)S(1)} fusion(f32[2048,256]{0,1:T(8,128)S(1)} %get-tuple-element.27, bf16[1,1,2048,2048]{3,2,1,0:T(8,128)(2,1)} %param.9), kind=kOutput, calls=%fused_computation.40 | convolution fusion | flops 2149056256 | bytes 10486784 | tf_op jit(solution)/shard_map/dot_general | solution.py:111
  483.1 6.0 %all-reduce.2 = (f32[256]{0:T(256)S(1)}, f32[256]{0:T(256)S(1)}) all-reduce(f32[256]{0:T(256)S(1)} %get-tuple-element.26, f32[256]{0:T(256)S(1)} %fusion.28), channel_id=1, replica_groups=mesh['row_0'=4,'row_1'=2,'col_0'=2,'col_1'=4,'col_2'=2] {'row_0'}, use_global_device_ids=true, to_apply=%region_20.22 | all-reduce | flops 512 | bytes 4096 | tf_op jit(solution)/shard_map/psum | solution.py:40
  489.1 5.3 %all-reduce.8 = (f32[256]{0:T(256)S(1)}, f32[256]{0:T(256)S(1)}) all-reduce(f32[256]{0:T(256)S(1)} %get-tuple-element.10, f32[256]{0:T(256)S(1)} %get-tuple-element.11), channel_id=1, replica_groups=mesh['row_0'=4,'row_1'=2,'col_0'=2,'col_1'=4,'col_2'=2] {'row_1'}, use_global_device_ids=true, to_apply=%region_21.23 | all-reduce | flops 512 | bytes 4096 | tf_op jit(solution)/shard_map/psum | solution.py:40
  494.4 4.4 all-reduce.6
  498.8 14.1 %all-reduce = (f32[256]{0:T(256)S(1)}, f32[256]{0:T(256)S(1)}) all-reduce(f32[256]{0:T(256)S(1)} %get-tuple-element.18, f32[256]{0:T(256)S(1)} %get-tuple-element.19), channel_id=1, replica_groups=mesh['row_0'=4,'row_1'=2,'col_0'=2,'col_1'=4,'col_2'=2] {'col_1'}, use_global_device_ids=true, to_apply=%region_23.25 | all-reduce | flops 512 | bytes 4096 | tf_op jit(solution)/shard_map/psum | solution.py:40
  512.9 6.4 %all-reduce.4 = (f32[256]{0:T(256)S(1)}, f32[256]{0:T(256)S(1)}) all-reduce(f32[256]{0:T(256)S(1)} %get-tuple-element.6, f32[256]{0:T(256)S(1)} %get-tuple-element.7), channel_id=1, replica_groups=mesh['row_0'=4,'row_1'=2,'col_0'=2,'col_1'=4,'col_2'=2] {'col_2'}, use_global_device_ids=true, to_apply=%region_24.26 | all-reduce | flops 512 | bytes 4096 | tf_op jit(solution)/shard_map/psum | solution.py:40
  519.2 3.0 fusion.26
  (77 shorter events, 42.2 us)
Async XLA Ops:
  0.0 135.4 %copy-start = (f32[512,256]{1,0:T(8,128)S(1)}, f32[512,256]{1,0:T(8,128)}, u32[]{:S(2)}) copy-start(f32[512,256]{1,0:T(8,128)} %param.12) | copy-start | bytes 1572868
  3.4 1.3 copy-start.3
  18.7 13.3 %copy-start.10 = (s32[1,1,4]{2,1,0:T(1,128)S(1)}, s32[1,1,4]{2,1,0:T(1,128)}, u32[]{:S(2)}) copy-start(s32[1,1,4]{2,1,0:T(1,128)} %param.14) | copy-start | bytes 52
  18.7 13.4 %copy-start.8 = (s32[1,1,4,512]{3,2,1,0:T(4,128)S(1)}, s32[1,1,4,512]{3,2,1,0:T(4,128)}, u32[]{:S(2)}) copy-start(s32[1,1,4,512]{3,2,1,0:T(4,128)} %param.13) | copy-start | bytes 24580
  18.8 16.1 %collective-permute-start = (f32[1,512,256]{2,1,0:T(8,128)S(1)}, f32[1,512,256]{2,1,0:T(8,128)S(1)}, u32[]{:S(2)}, u32[]{:S(2)}) collective-permute-start(f32[1,512,256]{2,1,0:T(8,128)S(1)} %get-tuple-element.42), channel_id=1, source_target_pairs={{0,16},{16,32},{32,48},{48,64},{64,80},{80,96},{96,112},{1,17},{17... | collective-permute-start | bytes 1572872 | tf_op jit(solution)/shard_map/ppermute | solution.py:19
  24.3 11.2 %collective-permute-start.3 = (f32[1,512,256]{2,1,0:T(8,128)S(1)}, f32[1,512,256]{2,1,0:T(8,128)S(1)}, u32[]{:S(2)}, u32[]{:S(2)}) collective-permute-start(f32[1,512,256]{2,1,0:T(8,128)S(1)} %get-tuple-element.43), channel_id=1, source_target_pairs={{1,0},{2,1},{3,2},{4,3},{5,4},{6,5},{7,6},{8,7},{9,8},{10,9},{11,1... | collective-permute-start | bytes 1572872 | tf_op jit(solution)/shard_map/ppermute | solution.py:22
  27.2 9.6 %collective-permute-start.2 = (f32[1,512,256]{2,1,0:T(8,128)S(1)}, f32[1,512,256]{2,1,0:T(8,128)S(1)}, u32[]{:S(2)}, u32[]{:S(2)}) collective-permute-start(f32[1,512,256]{2,1,0:T(8,128)S(1)} %get-tuple-element.44), channel_id=1, source_target_pairs={{0,1},{1,2},{2,3},{3,4},{4,5},{5,6},{6,7},{7,8},{8,9},{9,10},{10,1... | collective-permute-start | bytes 1572872 | tf_op jit(solution)/shard_map/ppermute | solution.py:19
  30.7 17.4 %collective-permute-start.1 = (f32[1,512,256]{2,1,0:T(8,128)S(1)}, f32[1,512,256]{2,1,0:T(8,128)S(1)}, u32[]{:S(2)}, u32[]{:S(2)}) collective-permute-start(f32[1,512,256]{2,1,0:T(8,128)S(1)} %get-tuple-element.45), channel_id=1, source_target_pairs={{16,0},{32,16},{48,32},{64,48},{80,64},{96,80},{112,96},{17,1},{33... | collective-permute-start | bytes 1572872 | tf_op jit(solution)/shard_map/ppermute | solution.py:22
  49.9 12.8 %copy-start.7 = (f32[1,1,32,2048]{3,2,1,0:T(8,128)S(1)}, f32[1,1,32,2048]{3,2,1,0:T(8,128)}, u32[]{:S(2)}) copy-start(f32[1,1,32,2048]{3,2,1,0:T(8,128)} %param.11) | copy-start | bytes 786436
  66.4 69.0 %all-to-all-start = ((f32[128,32,256]{2,1,0:T(8,128)}), f32[128,32,256]{2,1,0:T(8,128)}, u32[]{:S(2)}, u32[]{:S(2)}) async-start(f32[128,32,256]{2,1,0:T(8,128)} %stack.22), calls=%async_computation | async-start | bytes 8388608 | tf_op jit(solution)/shard_map/all_to_all | solution.py:85
  138.4 14.5 %all-to-all-start.1 = ((f32[16,32,256]{2,1,0:T(8,128)}), f32[16,32,256]{2,1,0:T(8,128)S(1)}, u32[]{:S(2)}, u32[]{:S(2)}) async-start(f32[16,32,256]{2,1,0:T(8,128)} %bitcast.118), calls=%async_computation.1 | async-start | bytes 1048576 | tf_op jit(solution)/shard_map/all_to_all | solution.py:35
  171.1 12.0 %copy-start.9 = (s32[1,1,2048]{2,1,0:T(1,128)S(1)}, s32[1,1,2048]{2,1,0:T(1,128)}, u32[]{:S(2)}) copy-start(s32[1,1,2048]{2,1,0:T(1,128)} %param.15) | copy-start | bytes 24580
  172.3 20.7 %collective-permute-start.4 = (f32[1,512,256]{2,1,0:T(8,128)}, f32[1,512,256]{2,1,0:T(8,128)}, u32[]{:S(2)}, u32[]{:S(2)}) collective-permute-start(f32[1,512,256]{2,1,0:T(8,128)} %get-tuple-element.38), channel_id=1, source_target_pairs={{0,16},{16,32},{32,48},{48,64},{64,80},{80,96},{96,112},{1,17},{17... | collective-permute-start | bytes 1572872 | tf_op jit(solution)/shard_map/ppermute | solution.py:19
  175.7 17.3 %collective-permute-start.7 = (f32[1,512,256]{2,1,0:T(8,128)}, f32[1,512,256]{2,1,0:T(8,128)}, u32[]{:S(2)}, u32[]{:S(2)}) collective-permute-start(f32[1,512,256]{2,1,0:T(8,128)} %get-tuple-element.39), channel_id=1, source_target_pairs={{1,0},{2,1},{3,2},{4,3},{5,4},{6,5},{7,6},{8,7},{9,8},{10,9},{11,1... | collective-permute-start | bytes 1572872 | tf_op jit(solution)/shard_map/ppermute | solution.py:22
  179.1 13.9 %collective-permute-start.6 = (f32[1,512,256]{2,1,0:T(8,128)}, f32[1,512,256]{2,1,0:T(8,128)}, u32[]{:S(2)}, u32[]{:S(2)}) collective-permute-start(f32[1,512,256]{2,1,0:T(8,128)} %get-tuple-element.40), channel_id=1, source_target_pairs={{0,1},{1,2},{2,3},{3,4},{4,5},{5,6},{6,7},{7,8},{8,9},{9,10},{10,1... | collective-permute-start | bytes 1572872 | tf_op jit(solution)/shard_map/ppermute | solution.py:19
  181.2 18.0 %collective-permute-start.5 = (f32[1,512,256]{2,1,0:T(8,128)S(1)}, f32[1,512,256]{2,1,0:T(8,128)}, u32[]{:S(2)}, u32[]{:S(2)}) collective-permute-start(f32[1,512,256]{2,1,0:T(8,128)S(1)} %get-tuple-element.41), channel_id=1, source_target_pairs={{16,0},{32,16},{48,32},{64,48},{80,64},{96,80},{112,96},{17,1},{33... | collective-permute-start | bytes 1572872 | tf_op jit(solution)/shard_map/ppermute | solution.py:22
  200.9 2.3 copy-start.1
  220.4 6.7 %copy-start.5 = (f32[2048,256]{0,1:T(8,128)}, f32[2048,256]{0,1:T(8,128)S(1)}, u32[]{:S(2)}) copy-start(f32[2048,256]{0,1:T(8,128)S(1)} %get-tuple-element.29) | copy-start | bytes 6291460
  220.4 42.9 %copy-start.4 = (f32[1,1,2048,256]{2,3,1,0:T(8,128)S(1)}, f32[1,1,2048,256]{2,3,1,0:T(8,128)}, u32[]{:S(2)}) copy-start(f32[1,1,2048,256]{2,3,1,0:T(8,128)} %copy-done.3) | copy-start | bytes 6291460
  283.6 15.1 %collective-permute-start.8 = (f32[1,512,256]{2,1,0:T(8,128)S(1)}, f32[1,512,256]{2,1,0:T(8,128)S(1)}, u32[]{:S(2)}, u32[]{:S(2)}) collective-permute-start(f32[1,512,256]{2,1,0:T(8,128)S(1)} %get-tuple-element.34), channel_id=1, source_target_pairs={{0,16},{16,32},{32,48},{48,64},{64,80},{80,96},{96,112},{1,17},{17... | collective-permute-start | bytes 1572872 | tf_op jit(solution)/shard_map/ppermute | solution.py:19
  287.9 11.0 %collective-permute-start.11 = (f32[1,512,256]{2,1,0:T(8,128)S(1)}, f32[1,512,256]{2,1,0:T(8,128)S(1)}, u32[]{:S(2)}, u32[]{:S(2)}) collective-permute-start(f32[1,512,256]{2,1,0:T(8,128)S(1)} %get-tuple-element.35), channel_id=1, source_target_pairs={{1,0},{2,1},{3,2},{4,3},{5,4},{6,5},{7,6},{8,7},{9,8},{10,9},{11,1... | collective-permute-start | bytes 1572872 | tf_op jit(solution)/shard_map/ppermute | solution.py:22
  290.4 9.6 %collective-permute-start.10 = (f32[1,512,256]{2,1,0:T(8,128)S(1)}, f32[1,512,256]{2,1,0:T(8,128)S(1)}, u32[]{:S(2)}, u32[]{:S(2)}) collective-permute-start(f32[1,512,256]{2,1,0:T(8,128)S(1)} %get-tuple-element.36), channel_id=1, source_target_pairs={{0,1},{1,2},{2,3},{3,4},{4,5},{5,6},{6,7},{7,8},{8,9},{9,10},{10,1... | collective-permute-start | bytes 1572872 | tf_op jit(solution)/shard_map/ppermute | solution.py:19
  293.9 18.7 %collective-permute-start.9 = (f32[1,512,256]{2,1,0:T(8,128)S(1)}, f32[1,512,256]{2,1,0:T(8,128)S(1)}, u32[]{:S(2)}, u32[]{:S(2)}) collective-permute-start(f32[1,512,256]{2,1,0:T(8,128)S(1)} %get-tuple-element.37), channel_id=1, source_target_pairs={{16,0},{32,16},{48,32},{64,48},{80,64},{96,80},{112,96},{17,1},{33... | collective-permute-start | bytes 1572872 | tf_op jit(solution)/shard_map/ppermute | solution.py:22
  428.1 12.9 %collective-permute-start.12 = (f32[1,512,256]{2,1,0:T(8,128)}, f32[1,512,256]{2,1,0:T(8,128)}, u32[]{:S(2)}, u32[]{:S(2)}) collective-permute-start(f32[1,512,256]{2,1,0:T(8,128)} %get-tuple-element.30), channel_id=1, source_target_pairs={{0,16},{16,32},{32,48},{48,64},{64,80},{80,96},{96,112},{1,17},{17... | collective-permute-start | bytes 1572872 | tf_op jit(solution)/shard_map/ppermute | solution.py:19
  431.5 10.8 %collective-permute-start.15 = (f32[1,512,256]{2,1,0:T(8,128)}, f32[1,512,256]{2,1,0:T(8,128)}, u32[]{:S(2)}, u32[]{:S(2)}) collective-permute-start(f32[1,512,256]{2,1,0:T(8,128)} %get-tuple-element.31), channel_id=1, source_target_pairs={{1,0},{2,1},{3,2},{4,3},{5,4},{6,5},{7,6},{8,7},{9,8},{10,9},{11,1... | collective-permute-start | bytes 1572872 | tf_op jit(solution)/shard_map/ppermute | solution.py:22
  435.0 8.5 %collective-permute-start.14 = (f32[1,512,256]{2,1,0:T(8,128)}, f32[1,512,256]{2,1,0:T(8,128)}, u32[]{:S(2)}, u32[]{:S(2)}) collective-permute-start(f32[1,512,256]{2,1,0:T(8,128)} %get-tuple-element.32), channel_id=1, source_target_pairs={{0,1},{1,2},{2,3},{3,4},{4,5},{5,6},{6,7},{7,8},{8,9},{9,10},{10,1... | collective-permute-start | bytes 1572872 | tf_op jit(solution)/shard_map/ppermute | solution.py:19
  437.1 18.0 %collective-permute-start.13 = (f32[1,512,256]{2,1,0:T(8,128)S(1)}, f32[1,512,256]{2,1,0:T(8,128)}, u32[]{:S(2)}, u32[]{:S(2)}) collective-permute-start(f32[1,512,256]{2,1,0:T(8,128)S(1)} %get-tuple-element.33), channel_id=1, source_target_pairs={{16,0},{32,16},{48,32},{64,48},{80,64},{96,80},{112,96},{17,1},{33... | collective-permute-start | bytes 1572872 | tf_op jit(solution)/shard_map/ppermute | solution.py:22
  456.8 2.3 copy-start.2
  476.4 6.7 %copy-start.6 = (f32[2048,256]{0,1:T(8,128)}, f32[2048,256]{0,1:T(8,128)S(1)}, u32[]{:S(2)}) copy-start(f32[2048,256]{0,1:T(8,128)S(1)} %get-tuple-element.27) | copy-start | bytes 6291460
